TPU v7x, 32 devices: a whole 2x2x4 slice. The times are simulated.
32 devices in a mesh: parts: 1, axial: 8 (over y, x, core), radial: 4 (over z).
Axes of the slice: x: 2, y: 2, z: 4, core: 2. Of those that a mesh axis runs over, the one named last changes fastest.
Arguments:
- inputs: bfloat16 [64, 64, 8192], P(None, 'radial', ('parts', 'axial')), may hold values from -6 to 6
- saved_pre: bfloat16 [64, 64, 8192], P(None, 'radial', ('parts', 'axial')), may hold values from -6 to 6
- cotangent: bfloat16 [64, 64, 8192], P(None, 'radial', ('parts', 'axial')), may hold values from -24 to 24
- pointwise_weight: bfloat16 [64, 64], replicated, may hold values from -0.75 to 0.75
- spectral_weight: bfloat16 [32, 256, 64, 128], P('radial', 'axial'), may hold values from -3 to 3
Outputs:
- input_grad: bfloat16 [64, 64, 8192], P(None, 'radial', ('parts', 'axial'))
- spectral_grad: float32 [32, 256, 64, 128], P('radial', ('parts', 'axial'))
- weight_grad: float32 [64, 64], P('parts')
All inputs are finite; a program needn't handle non-finite values.
Results may differ from a plain program's by a relative error of at most 0.0053.
Values may be sent and summed in bfloat16 or wider, within the bound.
No kernel may reach another device: no remote copies, remote signals or barrier semaphores. Data moves between devices by JAX's collectives and lax.ppermute only.
A program may use at most 128 MiB of HBM per device.

v0:
```python
import math
import jax
import jax.numpy as jnp
from jax import lax
from jax.sharding import PartitionSpec as P

KA = 256
KR = 32


def axial_table(first, count, modes, total):
    points = first + jnp.arange(count, dtype=jnp.int32)
    orders = jnp.arange(modes, dtype=jnp.int32)
    phase = (points[:, None] * orders[None, :] % total).astype(jnp.float32) * (
        2.0 * math.pi / total
    )
    return (
        jnp.stack([jnp.cos(phase), -jnp.sin(phase)], axis=2)
        .reshape(count, 2 * modes)
        .astype(jnp.bfloat16)
    )


def radial_table(count, rows_first, rows_count, kept, total):
    orders = jnp.arange(count, dtype=jnp.int32)
    freqs = orders + jnp.where(orders >= kept // 2, total - kept, 0).astype(jnp.int32)
    rows = rows_first + jnp.arange(rows_count, dtype=jnp.int32)
    phase = (freqs[:, None] * rows[None, :] % total).astype(jnp.float32) * (2.0 * math.pi / total)
    return (jnp.cos(phase), jnp.sin(phase))


def gelu_slope(pre):
    value = pre.astype(jnp.float32)
    return 0.5 * (1.0 + jax.scipy.special.erf(value / math.sqrt(2.0))) + value * jnp.exp(
        -0.5 * value * value
    ) / math.sqrt(2.0 * math.pi)


def to_modes(axial_part, cos_r, sin_r, own_ax, channels, rad_rows):
    split = axial_part.reshape(own_ax, 2, channels, rad_rows)
    real_in = split[:, 0]
    imag_in = split[:, 1]
    high = lax.Precision.HIGHEST
    real_out = jnp.einsum("qr,kcr->qkc", cos_r, real_in, precision=high) + jnp.einsum(
        "qr,kcr->qkc", sin_r, imag_in, precision=high
    )
    imag_out = jnp.einsum("qr,kcr->qkc", cos_r, imag_in, precision=high) - jnp.einsum(
        "qr,kcr->qkc", sin_r, real_in, precision=high
    )
    return (real_out, imag_out)


def body(inputs, saved_pre, cotangent, pointwise_weight, spectral_weight):
    high = lax.Precision.HIGHEST
    channels, rad_rows, ax_cols = inputs.shape
    n_axial = lax.axis_size("axial")
    n_radial = lax.axis_size("radial")
    ax_index = lax.axis_index("axial")
    rad_index = lax.axis_index("radial")
    axial_total = ax_cols * n_axial
    radial_total = rad_rows * n_radial
    own_ax = KA // n_axial
    grad_pre = (cotangent.astype(jnp.float32) * gelu_slope(saved_pre)).astype(jnp.bfloat16)
    table = axial_table(ax_index * ax_cols, ax_cols, KA, axial_total)
    columns = table
    part_in = jnp.einsum("cra,aj->jcr", inputs, columns, preferred_element_type=jnp.float32)
    part_grad = jnp.einsum("cra,aj->jcr", grad_pre, columns, preferred_element_type=jnp.float32)
    summed = lax.psum_scatter(
        jnp.concatenate(
            [
                part_in.reshape(2 * own_ax * lax.axis_size("axial"), -1),
                part_grad.reshape(2 * own_ax * lax.axis_size("axial"), -1),
            ],
            axis=1,
        ),
        "axial",
        scatter_dimension=0,
        tiled=True,
    )
    half = channels * rad_rows
    spec_in = summed[:, :half].reshape(2 * own_ax, channels, rad_rows)
    spec_grad = summed[:, half:].reshape(2 * own_ax, channels, rad_rows)
    cos_r, sin_r = radial_table(KR, rad_index * rad_rows, rad_rows, KR, radial_total)
    x_real, x_imag = to_modes(spec_in, cos_r, sin_r, own_ax, channels, rad_rows)
    g_real, g_imag = to_modes(spec_grad, cos_r, sin_r, own_ax, channels, rad_rows)
    stacked = jnp.stack([x_real, x_imag, g_real, g_imag], axis=1)
    owned = lax.psum_scatter(stacked, "radial", scatter_dimension=0, tiled=True)
    orders = ax_index * own_ax + jnp.arange(own_ax, dtype=jnp.int32)
    scales = jnp.where(orders == 0, 1.0, 2.0).astype(jnp.float32) / (radial_total * axial_total)
    x_real = owned[:, 0]
    x_imag = owned[:, 1]
    dy_real = owned[:, 2] * scales[None, :, None]
    dy_imag = owned[:, 3] * scales[None, :, None]
    grad_real = (
        x_real[..., :, None] * dy_real[..., None, :] + x_imag[..., :, None] * dy_imag[..., None, :]
    )
    grad_imag = (
        x_real[..., :, None] * dy_imag[..., None, :] - x_imag[..., :, None] * dy_real[..., None, :]
    )
    spectral_grad = jnp.concatenate([grad_real, grad_imag], axis=3)
    w_real = spectral_weight[..., :channels].astype(jnp.float32)
    w_imag = spectral_weight[..., channels:].astype(jnp.float32)
    dx_real = jnp.einsum("qkio,qko->qki", w_real, dy_real, precision=high) + jnp.einsum(
        "qkio,qko->qki", w_imag, dy_imag, precision=high
    )
    dx_imag = jnp.einsum("qkio,qko->qki", w_real, dy_imag, precision=high) - jnp.einsum(
        "qkio,qko->qki", w_imag, dy_real, precision=high
    )
    mode_grad = jnp.stack([dx_real, dx_imag], axis=1)
    row_first = rad_index * rad_rows
    piece = lax.all_gather(mode_grad, "radial", axis=0, tiled=True)
    cos_q, sin_q = radial_table(piece.shape[0], row_first, rad_rows, KR, radial_total)
    piece_real = piece[:, 0]
    piece_imag = piece[:, 1]
    out_real = jnp.einsum("qr,qkc->kcr", cos_q, piece_real, precision=high) - jnp.einsum(
        "qr,qkc->kcr", sin_q, piece_imag, precision=high
    )
    out_imag = jnp.einsum("qr,qkc->kcr", sin_q, piece_real, precision=high) + jnp.einsum(
        "qr,qkc->kcr", cos_q, piece_imag, precision=high
    )
    back = jnp.stack([out_real, out_imag], axis=1)
    lines_back = back.astype(jnp.bfloat16).reshape(2 * own_ax, channels * rad_rows)
    columns = table
    spectral_part = jnp.einsum(
        "jm,aj->ma",
        lax.all_gather(lines_back, "axial", axis=0, tiled=True),
        columns,
        preferred_element_type=jnp.float32,
    )
    flat_grad = grad_pre.reshape(channels, rad_rows * ax_cols)
    flat_in = inputs.reshape(channels, rad_rows * ax_cols)
    point_part = jnp.dot(pointwise_weight, flat_grad, preferred_element_type=jnp.float32)
    input_grad = (
        (point_part + spectral_part.reshape(channels, rad_rows * ax_cols))
        .astype(jnp.bfloat16)
        .reshape(channels, rad_rows, ax_cols)
    )
    local_weight = lax.dot_general(
        flat_in, flat_grad, (((1,), (1,)), ((), ())), preferred_element_type=jnp.float32
    )
    weight_grad = lax.psum(local_weight, ("axial", "radial")) / math.sqrt(
        radial_total * axial_total
    )
    return (input_grad, spectral_grad, weight_grad)


def solution(mesh):
    placed = (
        P(None, "radial", ("parts", "axial")),
        P(None, "radial", ("parts", "axial")),
        P(None, "radial", ("parts", "axial")),
        P(),
        P("radial", "axial", None, None),
    )
    return jax.shard_map(
        body,
        mesh=mesh,
        in_specs=placed,
        out_specs=(
            P(None, "radial", ("parts", "axial")),
            P("radial", ("parts", "axial"), None, None),
            P("parts", None),
        ),
        check_vma=False,
    )
```

profile of v0, /device:TPU:0, one launch (start us, length us, event | category | flops | bytes accessed | tf_op | source)
XLA Modules:
  0.0 311.8 jit_solution(6213764440670143054)
XLA Ops:
  7.2 5.0 %fusion.44 = (bf16[1024,256,1]{1,0,2:T(8,128)(2,1)S(1)}, bf16[1024,256,1]{1,0,2:T(8,128)(2,1)S(1)}) fusion(s32[1024]{0:T(1024)S(1)} %iota_add_fusion), kind=kLoop, calls=%fused_computation.67 | loop fusion | flops 4456448 | bytes 1052672 | tf_op jit(solution)/shard_map/cos | solution.py:18
  12.4 2.1 copy.31
  16.0 3.9 %fusion.9 = bf16[64,16,1024]{2,1,0:T(8,128)(2,1)S(1)} fusion(bf16[64,16,1024]{2,1,0:T(8,128)(2,1)} %param.6, bf16[64,16,1024]{2,1,0:T(8,128)(2,1)} %param.7), kind=kLoop, calls=%fused_computation.18 | loop fusion | flops 12582912 | bytes 6291456 | tf_op jit(solution)/shard_map/convert_element_type | solution.py:63
  22.5 2.5 pad_maximum_fusion.1
  25.7 53.6 %reduce-scatter.3.cloned.1.call-done = f32[64,2048]{1,0:T(8,128)} async-done(((f32[512,2048]{1,0:T(8,128)}), f32[64,2048]{1,0:T(8,128)}) %reduce-scatter.3.cloned.1.call-update) | async-done | bytes 524304 | tf_op jit(solution)/shard_map/reduce_scatter | solution.py:68
  80.3 2.0 reshape_reshape.6
  82.4 4.3 %fusion.41 = f32[32,32,64]{2,0,1:T(8,128)S(1)} fusion(f32[32,2,64,16]{3,2,1,0:T(8,128)} %reshape_reshape.6, s32[16]{0:T(128)S(1)} %iota_add_fusion.1, s32[32]{0:T(128)S(1)} %fusion.84), kind=kOutput, calls=%fused_computation.62 | convolution fusion | flops 12590080 | bytes 1310912 | tf_op jit(solution)/shard_map/qr,kcr->qkc/dot_general | solution.py:47
  86.7 4.3 %fusion.40 = f32[32,32,64]{2,0,1:T(8,128)S(1)} fusion(f32[32,2,64,16]{3,2,1,0:T(8,128)} %reshape_reshape.6, s32[16]{0:T(128)S(1)} %iota_add_fusion.1, s32[32]{0:T(128)S(1)} %fusion.84), kind=kOutput, calls=%fused_computation.61 | convolution fusion | flops 12590080 | bytes 1310912 | tf_op jit(solution)/shard_map/qr,kcr->qkc/dot_general | solution.py:44
  91.0 2.0 reshape_reshape.7
  93.1 4.5 %fusion.43 = f32[32,32,64]{2,0,1:T(8,128)S(1)} fusion(f32[32,2,64,16]{3,2,1,0:T(8,128)} %reshape_reshape.7, s32[16]{0:T(128)S(1)} %iota_add_fusion.1, s32[32]{0:T(128)S(1)} %fusion.84), kind=kOutput, calls=%fused_computation.64 | convolution fusion | flops 12590080 | bytes 1310912 | tf_op jit(solution)/shard_map/qr,kcr->qkc/dot_general | solution.py:47
  97.6 4.3 %fusion.42 = f32[32,32,64]{2,0,1:T(8,128)S(1)} fusion(f32[32,2,64,16]{3,2,1,0:T(8,128)} %reshape_reshape.7, s32[16]{0:T(128)S(1)} %iota_add_fusion.1, s32[32]{0:T(128)S(1)} %fusion.84), kind=kOutput, calls=%fused_computation.63 | convolution fusion | flops 12590080 | bytes 1310912 | tf_op jit(solution)/shard_map/qr,kcr->qkc/dot_general | solution.py:44
  101.9 4.4 %fusion.23 = f32[32,1,32,64]{3,0,2,1:T(8,128)S(1)} fusion(f32[32,32,64]{2,0,1:T(8,128)S(1)} %fusion.41, f32[32,2,64,16]{3,2,1,0:T(8,128)} %reshape_reshape.6, s32[16]{0:T(128)S(1)} %iota_add_fusion.1, s32[32]{0:T(128)S(1)} %fusion.84), kind=kOutput, calls=%fused_computation.40 | convolution fusion | flops 12655616 | bytes 1573056 | tf_op jit(solution)/shard_map/qr,kcr->qkc/dot_general | solution.py:47
  106.3 3.2 %fusion.24 = f32[32,1,32,64]{3,0,2,1:T(8,128)S(1)} fusion(f32[32,32,64]{2,0,1:T(8,128)S(1)} %fusion.40, f32[32,2,64,16]{3,2,1,0:T(8,128)S(1)} %copy-done.2, s32[16]{0:T(128)S(1)} %iota_add_fusion.1, s32[32]{0:T(128)S(1)} %fusion.84), kind=kOutput, calls=%fused_computation.42 | convolution fusion | flops 12655616 | bytes 1836032 | tf_op jit(solution)/shard_map/qr,kcr->qkc/dot_general | solution.py:44
  109.5 3.3 %fusion.21 = f32[32,1,32,64]{3,0,2,1:T(8,128)S(1)} fusion(f32[32,32,64]{2,0,1:T(8,128)S(1)} %fusion.43, f32[32,2,64,16]{3,2,1,0:T(8,128)S(1)} %copy-done.3, s32[16]{0:T(128)S(1)} %iota_add_fusion.1, s32[32]{0:T(128)S(1)} %fusion.84), kind=kOutput, calls=%fused_computation.36 | convolution fusion | flops 12655616 | bytes 1836032 | tf_op jit(solution)/shard_map/qr,kcr->qkc/dot_general | solution.py:47
  112.8 3.1 %fusion.22 = f32[32,1,32,64]{3,0,2,1:T(8,128)S(1)} fusion(f32[32,32,64]{2,0,1:T(8,128)S(1)} %fusion.42, f32[32,2,64,16]{3,2,1,0:T(8,128)S(1)} %copy-done.3, s32[16]{0:T(128)S(1)} %iota_add_fusion.1, s32[32]{0:T(128)S(1)} %fusion.84), kind=kOutput, calls=%fused_computation.38 | convolution fusion | flops 12655616 | bytes 1836032 | tf_op jit(solution)/shard_map/qr,kcr->qkc/dot_general | solution.py:44
  115.9 1.6 pad_maximum_fusion.2
  117.6 44.0 %reduce-scatter.5.cloned.1.call-done = f32[8,4,32,64]{3,0,2,1:T(8,128)} async-done(((f32[32,4,32,64]{3,0,2,1:T(8,128)}), f32[8,4,32,64]{3,0,2,1:T(8,128)}) %reduce-scatter.5.cloned.1.call-update) | async-done | bytes 262160 | tf_op jit(solution)/shard_map/reduce_scatter | solution.py:87
  162.8 8.6 %fusion.10 = f32[8,32,1,64]{3,2,1,0:T(1,128)S(1)} fusion(bf16[8,32,64,128]{3,2,1,0:T(8,128)(2,1)} %param.9, f32[8,32,64,1]{2,0,1,3:T(8,128)S(1)} %bitcast.134), kind=kOutput, calls=%fused_computation.19 | convolution fusion | flops 12582912 | bytes 4325376 | tf_op jit(solution)/shard_map/qkio,qko->qki/dot_general | solution.py:106
  171.4 6.6 %fusion.16 = f32[8,32,1,64]{3,2,1,0:T(1,128)S(1)} fusion(bf16[8,32,64,128]{3,2,1,0:T(8,128)(2,1)S(1)} %copy-done.11, f32[8,32,64,1]{2,0,1,3:T(8,128)S(1)} %bitcast.135), kind=kOutput, calls=%fused_computation.25 | convolution fusion | flops 12582912 | bytes 4325376 | tf_op jit(solution)/shard_map/qkio,qko->qki/dot_general | solution.py:103
  178.0 6.6 %fusion.14 = f32[8,32,1,64]{3,2,1,0:T(1,128)S(1)} fusion(bf16[8,32,64,128]{3,2,1,0:T(8,128)(2,1)S(1)} %copy-done.11, f32[8,32,64,1]{2,0,1,3:T(8,128)S(1)} %bitcast.136), kind=kOutput, calls=%fused_computation.23 | convolution fusion | flops 12582912 | bytes 4325376 | tf_op jit(solution)/shard_map/qkio,qko->qki/dot_general | solution.py:106
  184.6 6.7 %fusion.12 = f32[8,32,1,64]{3,2,1,0:T(1,128)S(1)} fusion(bf16[8,32,64,128]{3,2,1,0:T(8,128)(2,1)S(1)} %copy-done.11, f32[8,32,64,1]{2,0,1,3:T(8,128)S(1)} %bitcast.137), kind=kOutput, calls=%fused_computation.21 | convolution fusion | flops 12582912 | bytes 4325376 | tf_op jit(solution)/shard_map/qkio,qko->qki/dot_general | solution.py:103
  191.6 21.4 %all_gather.6 = f32[32,2,32,64]{3,0,2,1:T(8,128)S(1)} all-gather(f32[8,2,32,64]{3,0,2,1:T(8,128)S(1)} %pad_maximum_fusion.3), channel_id=1, replica_groups=mesh['parts'=1,'axial'=8,'radial'=4] {'radial'}, dimensions={0}, use_global_device_ids=true | all-gather | bytes 655360 | tf_op jit(solution)/shard_map/all_gather | solution.py:111
  215.6 2.4 convert_element_type.61
  218.1 6.1 %fusion.29 = f32[64,64]{0,1:T(8,128)S(1)} fusion(bf16[64,16,1024]{2,1,0:T(8,128)(2,1)S(1)} %copy-done, bf16[64,16,1024]{2,1,0:T(8,128)(2,1)} %copy-done.4), kind=kOutput, calls=%fused_computation.49 | convolution fusion | flops 134217728 | bytes 4210688 | tf_op jit(solution)/shard_map/dot_general | solution.py:138
  224.1 39.3 %psum.7 = f32[64,64]{0,1:T(8,128)S(1)} all-reduce(f32[64,64]{0,1:T(8,128)S(1)} %fusion.29), channel_id=1, replica_groups=mesh['parts'=1,'axial'=8,'radial'=4] {'axial','radial'}, use_global_device_ids=true, to_apply=%region_2.3 | all-reduce | flops 4096 | bytes 32768 | tf_op jit(solution)/shard_map/psum | solution.py:141
  264.1 4.2 %copy.54 = bf16[8,8,16,1024]{3,1,2,0:T(8,128)(2,1)} copy(bf16[8,8,16,1024]{3,2,1,0:T(8,128)(2,1)} %bitcast.130) | data formatting | bytes 4194304
  268.5 8.5 %multiply_add_fusion = (f32[8,32,64,64]{3,2,1,0:T(8,128)}, f32[8,32,64,64]{3,2,1,0:T(8,128)}) fusion(f32[8,32,64]{2,1,0:T(8,128)S(1)} %copy.40, f32[8,32,64]{2,1,0:T(8,128)S(1)} %copy.39, f32[8,32,64]{2,1,0:T(8,128)S(1)} %copy.38, f32[8,32,64]{2,1,0:T(8,128)S(1)} %copy.37), kind=kLoop, calls=%fused_computation.5 | loop fusion | flops 6291456 | bytes 8650752 | tf_op jit(solution)/shard_map/add | solution.py:95
  277.0 12.2 %pad_maximum_fusion = f32[8,32,64,128]{3,2,1,0:T(8,128)} fusion(f32[8,32,64,64]{3,2,1,0:T(8,128)} %get-tuple-element.15, f32[8,32,64,64]{3,2,1,0:T(8,128)} %get-tuple-element.14), kind=kLoop, calls=%fused_computation.3 | loop fusion | flops 2097152 | bytes 16777216 | tf_op jit(solution)/shard_map/concatenate | solution.py:100
  289.2 4.5 %fusion.137 = f32[1024,1024]{1,0:T(8,128)} fusion(bf16[512,1024]{1,0:T(8,128)(2,1)} %all-gather.2.cloned.1.call-done, bf16[1024,512]{0,1:T(8,128)(2,1)S(1)} %copy-done.6), kind=kOutput, calls=%fused_computation.166 | convolution fusion | flops 1073741824 | bytes 6291456 | tf_op jit(solution)/shard_map/jm,aj->ma/dot_general | solution.py:124
  293.7 5.0 %reshape.173 = f32[64,16384]{1,0:T(8,128)} reshape(f32[1024,1024]{1,0:T(8,128)} %fusion.137) | data formatting | bytes 8388608 | tf_op jit(solution)/shard_map/reshape | solution.py:134
  298.7 3.7 %fusion.1 = bf16[64,16384]{1,0:T(8,128)(2,1)S(1)} fusion(f32[64,16384]{1,0:T(8,128)} %reshape.173, bf16[64,64]{1,0:T(8,128)(2,1)S(1)} %copy-done.10, bf16[64,16384]{1,0:T(8,128)(2,1)} %bitcast.131), kind=kOutput, calls=%fused_computation.2 | convolution fusion | flops 136314880 | bytes 8396800 | tf_op jit(solution)/shard_map/dot_general | solution.py:132
  302.3 2.5 copy.55
  (56 shorter events, 10.9 us)
Async XLA Ops:
  7.2 14.1 %copy-start = (bf16[64,16,1024]{2,1,0:T(8,128)(2,1)S(1)}, bf16[64,16,1024]{2,1,0:T(8,128)(2,1)}, u32[]{:S(2)}) copy-start(bf16[64,16,1024]{2,1,0:T(8,128)(2,1)} %param.5) | copy-start | bytes 6291460
  7.2 72.1 %reduce-scatter.3.cloned.1.call-start = ((), (), s32[]{:S(2)}) async-start(), calls=%async_computation.2 | async-start | bytes 4718592 | tf_op jit(solution)/shard_map/reduce_scatter | solution.py:68
  16.0 5.3 %copy-start.5 = (bf16[1024,512]{0,1:T(8,128)(2,1)}, bf16[1024,512]{0,1:T(8,128)(2,1)S(1)}, u32[]{:S(2)}) copy-start(bf16[1024,512]{0,1:T(8,128)(2,1)S(1)} %convert_element_type.60) | copy-start | bytes 3145732
  19.9 1.3 copy-start.4
  25.1 136.5 %reduce-scatter.5.cloned.1.call-start = ((), (), s32[]{:S(2)}) async-start(), calls=%async_computation.3 | async-start | bytes 2621440 | tf_op jit(solution)/shard_map/reduce_scatter | solution.py:87
  93.1 13.2 %copy-start.2 = (f32[32,2,64,16]{3,2,1,0:T(8,128)S(1)}, f32[32,2,64,16]{3,2,1,0:T(8,128)}, u32[]{:S(2)}) copy-start(f32[32,2,64,16]{3,2,1,0:T(8,128)} %reshape_reshape.6) | copy-start | bytes 786436
  93.1 16.4 %copy-start.3 = (f32[32,2,64,16]{3,2,1,0:T(8,128)S(1)}, f32[32,2,64,16]{3,2,1,0:T(8,128)}, u32[]{:S(2)}) copy-start(f32[32,2,64,16]{3,2,1,0:T(8,128)} %reshape_reshape.7) | copy-start | bytes 786436
  117.5 171.7 %all-gather.2.cloned.1.call-start = ((), (), s32[]{:S(2)}) async-start(), calls=%async_computation.4 | async-start | bytes 1179648 | tf_op jit(solution)/shard_map/all_gather | solution.py:126
  161.5 9.9 %copy-start.11 = (bf16[8,32,64,128]{3,2,1,0:T(8,128)(2,1)S(1)}, bf16[8,32,64,128]{3,2,1,0:T(8,128)(2,1)}, u32[]{:S(2)}) copy-start(bf16[8,32,64,128]{3,2,1,0:T(8,128)(2,1)} %param.9) | copy-start | bytes 12582916
  162.8 21.8 %copy-start.7 = (f32[8,32,64]{2,0,1:T(8,128)}, f32[8,32,64]{2,0,1:T(8,128)S(1)}, u32[]{:S(2)}) copy-start(f32[8,32,64]{2,0,1:T(8,128)S(1)} %get-tuple-element.12) | copy-start | bytes 196612
  218.0 50.3 %copy-start.8 = (f32[8,32,64]{2,0,1:T(8,128)S(1)}, f32[8,32,64]{2,0,1:T(8,128)}, u32[]{:S(2)}) copy-start(f32[8,32,64]{2,0,1:T(8,128)} %copy-done.7) | copy-start | bytes 196612
  218.0 50.4 %copy-start.9 = (f32[8,4,32,64]{3,0,2,1:T(8,128)S(1)}, f32[8,4,32,64]{3,0,2,1:T(8,128)}, u32[]{:S(2)}) copy-start(f32[8,4,32,64]{3,0,2,1:T(8,128)} %reduce-scatter.5.cloned.1.call-done) | copy-start | bytes 786436
  277.0 12.2 %copy-start.6 = (bf16[1024,512]{0,1:T(8,128)(2,1)S(1)}, bf16[1024,512]{0,1:T(8,128)(2,1)}, u32[]{:S(2)}) copy-start(bf16[1024,512]{0,1:T(8,128)(2,1)} %copy-done.5) | copy-start | bytes 3145732
  293.7 5.0 %copy-start.10 = (bf16[64,64]{1,0:T(8,128)(2,1)S(1)}, bf16[64,64]{1,0:T(8,128)(2,1)}, u32[]{:S(2)}) copy-start(bf16[64,64]{1,0:T(8,128)(2,1)} %param.8) | copy-start | bytes 24580
  298.7 6.2 %copy-start.1 = (bf16[64,16,1024]{2,1,0:T(8,128)(2,1)S(1)}, bf16[64,16,1024]{2,1,0:T(8,128)(2,1)}, u32[]{:S(2)}) copy-start(bf16[64,16,1024]{2,1,0:T(8,128)(2,1)} %param.5) | copy-start | bytes 6291460
Sparse Core Ops, SparseCore 0:
  25.2 53.9 reduce-scatter.2
  117.6 43.8 reduce-scatter.4
  218.2 23.7 all-gather.1
where the time goes:
time: 316 us; the launch traced here: 312 us
  waiting for transfers between devices  97.6 us (31%)
  matrix products  78.7 us (25%)
  blocking collectives  60.7 us (19%)
  other arithmetic  35.4 us (11%)
  local copies, waits for them, and re-layouts  24.2 us (8%)
  between operations  14.6 us (5%)
    reduce_scatter x1, waiting for transfers between devices, body(): lax.psum_scatter(jnp.concatenate([part_in.reshape(2 * own_ax * lax.axis_s...  53.6 us
    reduce_scatter x1, waiting for transfers between devices, body(): owned = lax.psum_scatter(stacked, 'radial', scatter_dimension=0, tiled=True)  44 us
    psum x1, blocking collectives, body(): lax.psum(local_weight, ('axial', 'radial'))  39.3 us
    all_gather x1, blocking collectives, body(): piece = lax.all_gather(mode_grad, 'radial', axis=0, tiled=True)  21.4 us
    concatenate x1, other arithmetic, body(): spectral_grad = jnp.concatenate([grad_real, grad_imag], axis=3)  12.2 us
    dot_general x2, matrix products, to_modes(): jnp.einsum('qr,kcr->qkc', cos_r, imag_in, precision=high)  8.82 us
    dot_general x2, matrix products, to_modes(): jnp.einsum('qr,kcr->qkc', cos_r, real_in, precision=high)  8.67 us
    dot_general x1, matrix products, body(): jnp.einsum('qkio,qko->qki', w_imag, dy_real, precision=high)  8.64 us
  transfers between devices with their start and end apart: 3, of which 2 were waited for; matrix products, arithmetic and copies ran while one was open for 10% of the time, Pallas kernels for 0%

commit v1 on v0

--- a/solution.py
+++ b/solution.py
@@ -6,6 +6,16 @@
 
 KA = 256
 KR = 32
+
+
+def gather_around(x, axis, dim):
+    ways, here, step = (lax.axis_size(axis), lax.axis_index(axis), x.shape[dim])
+    shape = [n * ways if d == dim else n for d, n in enumerate(x.shape)]
+    full = lax.dynamic_update_slice_in_dim(jnp.zeros(shape, x.dtype), x, here * step, axis=dim)
+    for far in range(1, ways):
+        x = lax.ppermute(x, axis, [(d, (d + 1) % ways) for d in range(ways)])
+        full = lax.dynamic_update_slice_in_dim(full, x, (here - far) % ways * step, axis=dim)
+    return full
 
 
 def axial_table(first, count, modes, total):
@@ -108,7 +118,7 @@
     )
     mode_grad = jnp.stack([dx_real, dx_imag], axis=1)
     row_first = rad_index * rad_rows
-    piece = lax.all_gather(mode_grad, "radial", axis=0, tiled=True)
+    piece = gather_around(mode_grad, "radial", 0)
     cos_q, sin_q = radial_table(piece.shape[0], row_first, rad_rows, KR, radial_total)
     piece_real = piece[:, 0]
     piece_imag = piece[:, 1]

time: 316 us -> 322 us (1.019)
  waiting for transfers between devices: 97.6 us -> 123 us
  blocking collectives: 60.7 us -> 38.2 us
    ppermute x0 -> x3, waiting for transfers between devices: none -> 25.8 us  [gather_around(): x = lax.ppermute(x, axis, [(d, (d + 1) % ways) for d in range(ways)])]
    all_gather x1 -> x0, blocking collectives: 21.4 us -> none  [body(): piece = lax.all_gather(mode_grad, 'radial', axis=0, tiled=True)]
  transfers between devices with their start and end apart: 3 -> 6, of which waited for: 2 -> 5; matrix products, arithmetic and copies ran while one was open for 10% -> 10% of each run, Pallas kernels for 0% -> 0%
where the time goes in v1:
time: 322 us; the launch traced here: 317 us
  waiting for transfers between devices  123 us (38%)
  matrix products  78.7 us (24%)
  blocking collectives  38.2 us (12%)
  other arithmetic  35.5 us (11%)
  local copies, waits for them, and re-layouts  25.4 us (8%)
  between operations  14.7 us (5%)
    reduce_scatter x1, waiting for transfers between devices, body(): lax.psum_scatter(jnp.concatenate([part_in.reshape(2 * own_ax * lax.axis_s...  53.6 us
    reduce_scatter x1, waiting for transfers between devices, body(): owned = lax.psum_scatter(stacked, 'radial', scatter_dimension=0, tiled=True)  43.9 us
    psum x1, blocking collectives, body(): lax.psum(local_weight, ('axial', 'radial'))  38.2 us
    ppermute x3, waiting for transfers between devices, gather_around(): x = lax.ppermute(x, axis, [(d, (d + 1) % ways) for d in range(ways)])  25.8 us
    concatenate x1, other arithmetic, body(): spectral_grad = jnp.concatenate([grad_real, grad_imag], axis=3)  12.2 us
    dot_general x2, matrix products, to_modes(): jnp.einsum('qr,kcr->qkc', cos_r, imag_in, precision=high)  8.82 us
    dot_general x2, matrix products, to_modes(): jnp.einsum('qr,kcr->qkc', cos_r, real_in, precision=high)  8.67 us
    dot_general x1, matrix products, body(): jnp.einsum('qkio,qko->qki', w_imag, dy_real, precision=high)  8.64 us
  transfers between devices with their start and end apart: 6, of which 5 were waited for; matrix products, arithmetic and copies ran while one was open for 10% of the time, Pallas kernels for 0%

profile of v1, /device:TPU:0, one launch (start us, length us, event | category | flops | bytes accessed | tf_op | source)
XLA Modules:
  0.0 316.7 jit_solution(664023375269989769)
XLA Ops:
  7.2 5.0 %fusion.44 = (bf16[1024,256,1]{1,0,2:T(8,128)(2,1)S(1)}, bf16[1024,256,1]{1,0,2:T(8,128)(2,1)S(1)}) fusion(s32[1024]{0:T(1024)S(1)} %iota_add_fusion), kind=kLoop, calls=%fused_computation.67 | loop fusion | flops 4456448 | bytes 1052672 | tf_op jit(solution)/shard_map/cos | solution.py:28
  12.4 2.1 copy.31
  16.0 3.9 %fusion.9 = bf16[64,16,1024]{2,1,0:T(8,128)(2,1)S(1)} fusion(bf16[64,16,1024]{2,1,0:T(8,128)(2,1)} %param.6, bf16[64,16,1024]{2,1,0:T(8,128)(2,1)} %param.7), kind=kLoop, calls=%fused_computation.18 | loop fusion | flops 12582912 | bytes 6291456 | tf_op jit(solution)/shard_map/convert_element_type | solution.py:73
  22.5 2.5 pad_maximum_fusion.1
  25.7 53.6 %reduce-scatter.3.cloned.1.call-done = f32[64,2048]{1,0:T(8,128)} async-done(((f32[512,2048]{1,0:T(8,128)}), f32[64,2048]{1,0:T(8,128)}) %reduce-scatter.3.cloned.1.call-update) | async-done | bytes 524304 | tf_op jit(solution)/shard_map/reduce_scatter | solution.py:78
  82.4 4.3 %fusion.41 = f32[32,32,64]{2,0,1:T(8,128)S(1)} fusion(f32[32,2,64,16]{3,2,1,0:T(8,128)} %reshape_reshape.6, s32[16]{0:T(128)S(1)} %iota_add_fusion.1, s32[32]{0:T(128)S(1)} %fusion.96), kind=kOutput, calls=%fused_computation.62 | convolution fusion | flops 12590080 | bytes 1310912 | tf_op jit(solution)/shard_map/qr,kcr->qkc/dot_general | solution.py:57
  86.7 4.3 %fusion.40 = f32[32,32,64]{2,0,1:T(8,128)S(1)} fusion(f32[32,2,64,16]{3,2,1,0:T(8,128)} %reshape_reshape.6, s32[16]{0:T(128)S(1)} %iota_add_fusion.1, s32[32]{0:T(128)S(1)} %fusion.96), kind=kOutput, calls=%fused_computation.61 | convolution fusion | flops 12590080 | bytes 1310912 | tf_op jit(solution)/shard_map/qr,kcr->qkc/dot_general | solution.py:54
  91.1 2.0 reshape_reshape.7
  93.1 4.5 %fusion.43 = f32[32,32,64]{2,0,1:T(8,128)S(1)} fusion(f32[32,2,64,16]{3,2,1,0:T(8,128)} %reshape_reshape.7, s32[16]{0:T(128)S(1)} %iota_add_fusion.1, s32[32]{0:T(128)S(1)} %fusion.96), kind=kOutput, calls=%fused_computation.64 | convolution fusion | flops 12590080 | bytes 1310912 | tf_op jit(solution)/shard_map/qr,kcr->qkc/dot_general | solution.py:57
  97.6 4.3 %fusion.42 = f32[32,32,64]{2,0,1:T(8,128)S(1)} fusion(f32[32,2,64,16]{3,2,1,0:T(8,128)} %reshape_reshape.7, s32[16]{0:T(128)S(1)} %iota_add_fusion.1, s32[32]{0:T(128)S(1)} %fusion.96), kind=kOutput, calls=%fused_computation.63 | convolution fusion | flops 12590080 | bytes 1310912 | tf_op jit(solution)/shard_map/qr,kcr->qkc/dot_general | solution.py:54
  101.9 4.4 %fusion.23 = f32[32,1,32,64]{3,0,2,1:T(8,128)S(1)} fusion(f32[32,32,64]{2,0,1:T(8,128)S(1)} %fusion.41, f32[32,2,64,16]{3,2,1,0:T(8,128)} %reshape_reshape.6, s32[16]{0:T(128)S(1)} %iota_add_fusion.1, s32[32]{0:T(128)S(1)} %fusion.96), kind=kOutput, calls=%fused_computation.40 | convolution fusion | flops 12655616 | bytes 1573056 | tf_op jit(solution)/shard_map/qr,kcr->qkc/dot_general | solution.py:57
  106.3 3.2 fusion.24
  109.5 3.3 %fusion.21 = f32[32,1,32,64]{3,0,2,1:T(8,128)S(1)} fusion(f32[32,32,64]{2,0,1:T(8,128)S(1)} %fusion.43, f32[32,2,64,16]{3,2,1,0:T(8,128)S(1)} %copy-done.3, s32[16]{0:T(128)S(1)} %iota_add_fusion.1, s32[32]{0:T(128)S(1)} %fusion.96), kind=kOutput, calls=%fused_computation.36 | convolution fusion | flops 12655616 | bytes 1836032 | tf_op jit(solution)/shard_map/qr,kcr->qkc/dot_general | solution.py:57
  112.8 3.1 fusion.22
  117.6 43.9 %reduce-scatter.5.cloned.1.call-done = f32[8,4,32,64]{3,0,2,1:T(8,128)} async-done(((f32[32,4,32,64]{3,0,2,1:T(8,128)}), f32[8,4,32,64]{3,0,2,1:T(8,128)}) %reduce-scatter.5.cloned.1.call-update) | async-done | bytes 262160 | tf_op jit(solution)/shard_map/reduce_scatter | solution.py:97
  162.8 8.6 %fusion.10 = f32[8,32,1,64]{3,2,1,0:T(1,128)S(1)} fusion(bf16[8,32,64,128]{3,2,1,0:T(8,128)(2,1)} %param.9, f32[8,32,64,1]{2,0,1,3:T(8,128)S(1)} %bitcast.134), kind=kOutput, calls=%fused_computation.19 | convolution fusion | flops 12582912 | bytes 4325376 | tf_op jit(solution)/shard_map/qkio,qko->qki/dot_general | solution.py:116
  171.4 6.6 %fusion.16 = f32[8,32,1,64]{3,2,1,0:T(1,128)S(1)} fusion(bf16[8,32,64,128]{3,2,1,0:T(8,128)(2,1)S(1)} %copy-done.11, f32[8,32,64,1]{2,0,1,3:T(8,128)S(1)} %bitcast.135), kind=kOutput, calls=%fused_computation.25 | convolution fusion | flops 12582912 | bytes 4325376 | tf_op jit(solution)/shard_map/qkio,qko->qki/dot_general | solution.py:113
  178.0 6.6 %fusion.14 = f32[8,32,1,64]{3,2,1,0:T(1,128)S(1)} fusion(bf16[8,32,64,128]{3,2,1,0:T(8,128)(2,1)S(1)} %copy-done.11, f32[8,32,64,1]{2,0,1,3:T(8,128)S(1)} %bitcast.136), kind=kOutput, calls=%fused_computation.23 | convolution fusion | flops 12582912 | bytes 4325376 | tf_op jit(solution)/shard_map/qkio,qko->qki/dot_general | solution.py:116
  184.6 6.7 %fusion.12 = f32[8,32,1,64]{3,2,1,0:T(1,128)S(1)} fusion(bf16[8,32,64,128]{3,2,1,0:T(8,128)(2,1)S(1)} %copy-done.11, f32[8,32,64,1]{2,0,1,3:T(8,128)S(1)} %bitcast.137), kind=kOutput, calls=%fused_computation.21 | convolution fusion | flops 12582912 | bytes 4325376 | tf_op jit(solution)/shard_map/qkio,qko->qki/dot_general | solution.py:113
  191.8 9.7 %collective-permute-done = f32[8,2,32,64]{3,0,2,1:T(8,128)S(1)} collective-permute-done((f32[8,2,32,64]{3,0,2,1:T(8,128)S(1)}, f32[8,2,32,64]{3,0,2,1:T(8,128)S(1)}, u32[]{:S(2)}, u32[]{:S(2)}) %collective-permute-start) | collective-permute-done | bytes 131104 | tf_op jit(solution)/shard_map/ppermute | solution.py:16
  201.8 8.8 %collective-permute-done.1 = f32[8,2,32,64]{3,0,2,1:T(8,128)} collective-permute-done((f32[8,2,32,64]{3,0,2,1:T(8,128)S(1)}, f32[8,2,32,64]{3,0,2,1:T(8,128)}, u32[]{:S(2)}, u32[]{:S(2)}) %collective-permute-start.1) | collective-permute-done | bytes 131104 | tf_op jit(solution)/shard_map/ppermute | solution.py:16
  211.7 7.3 %collective-permute-done.2 = f32[8,2,32,64]{3,0,2,1:T(8,128)S(1)} collective-permute-done((f32[8,2,32,64]{3,0,2,1:T(8,128)}, f32[8,2,32,64]{3,0,2,1:T(8,128)S(1)}, u32[]{:S(2)}, u32[]{:S(2)}) %collective-permute-start.2) | collective-permute-done | bytes 131104 | tf_op jit(solution)/shard_map/ppermute | solution.py:16
  221.6 2.4 convert_element_type.61
  224.1 6.1 %fusion.29 = f32[64,64]{0,1:T(8,128)S(1)} fusion(bf16[64,16,1024]{2,1,0:T(8,128)(2,1)S(1)} %copy-done, bf16[64,16,1024]{2,1,0:T(8,128)(2,1)} %copy-done.4), kind=kOutput, calls=%fused_computation.49 | convolution fusion | flops 134217728 | bytes 4210688 | tf_op jit(solution)/shard_map/dot_general | solution.py:148
  230.1 38.2 %psum.7 = f32[64,64]{0,1:T(8,128)S(1)} all-reduce(f32[64,64]{0,1:T(8,128)S(1)} %fusion.29), channel_id=1, replica_groups=mesh['parts'=1,'axial'=8,'radial'=4] {'axial','radial'}, use_global_device_ids=true, to_apply=%region_2.3 | all-reduce | flops 4096 | bytes 32768 | tf_op jit(solution)/shard_map/psum | solution.py:151
  269.0 4.2 %copy.54 = bf16[8,8,16,1024]{3,1,2,0:T(8,128)(2,1)} copy(bf16[8,8,16,1024]{3,2,1,0:T(8,128)(2,1)} %bitcast.130) | data formatting | bytes 4194304
  273.4 8.5 %multiply_add_fusion = (f32[8,32,64,64]{3,2,1,0:T(8,128)}, f32[8,32,64,64]{3,2,1,0:T(8,128)}) fusion(f32[8,32,64]{2,1,0:T(8,128)S(1)} %copy.40, f32[8,32,64]{2,1,0:T(8,128)S(1)} %copy.39, f32[8,32,64]{2,1,0:T(8,128)S(1)} %copy.38, f32[8,32,64]{2,1,0:T(8,128)S(1)} %copy.37), kind=kLoop, calls=%fused_computation.5 | loop fusion | flops 6291456 | bytes 8650752 | tf_op jit(solution)/shard_map/add | solution.py:105
  281.9 12.2 %pad_maximum_fusion = f32[8,32,64,128]{3,2,1,0:T(8,128)} fusion(f32[8,32,64,64]{3,2,1,0:T(8,128)} %get-tuple-element.15, f32[8,32,64,64]{3,2,1,0:T(8,128)} %get-tuple-element.14), kind=kLoop, calls=%fused_computation.3 | loop fusion | flops 2097152 | bytes 16777216 | tf_op jit(solution)/shard_map/concatenate | solution.py:110
  294.1 4.5 %fusion.137 = f32[1024,1024]{1,0:T(8,128)} fusion(bf16[512,1024]{1,0:T(8,128)(2,1)} %all-gather.2.cloned.1.call-done, bf16[1024,512]{0,1:T(8,128)(2,1)S(1)} %copy-done.6), kind=kOutput, calls=%fused_computation.170 | convolution fusion | flops 1073741824 | bytes 6291456 | tf_op jit(solution)/shard_map/jm,aj->ma/dot_general | solution.py:134
  298.5 5.0 %reshape.173 = f32[64,16384]{1,0:T(8,128)} reshape(f32[1024,1024]{1,0:T(8,128)} %fusion.137) | data formatting | bytes 8388608 | tf_op jit(solution)/shard_map/reshape | solution.py:144
  303.6 3.7 %fusion.1 = bf16[64,16384]{1,0:T(8,128)(2,1)S(1)} fusion(f32[64,16384]{1,0:T(8,128)} %reshape.173, bf16[64,64]{1,0:T(8,128)(2,1)S(1)} %copy-done.10, bf16[64,16384]{1,0:T(8,128)(2,1)} %bitcast.131), kind=kOutput, calls=%fused_computation.2 | convolution fusion | flops 136314880 | bytes 8396800 | tf_op jit(solution)/shard_map/dot_general | solution.py:142
  307.2 2.5 copy.55
  (65 shorter events, 15.9 us)
Async XLA Ops:
  7.2 14.1 %copy-start = (bf16[64,16,1024]{2,1,0:T(8,128)(2,1)S(1)}, bf16[64,16,1024]{2,1,0:T(8,128)(2,1)}, u32[]{:S(2)}) copy-start(bf16[64,16,1024]{2,1,0:T(8,128)(2,1)} %param.5) | copy-start | bytes 6291460
  7.2 72.1 %reduce-scatter.3.cloned.1.call-start = ((), (), s32[]{:S(2)}) async-start(), calls=%async_computation.2 | async-start | bytes 4718592 | tf_op jit(solution)/shard_map/reduce_scatter | solution.py:78
  16.0 5.3 %copy-start.5 = (bf16[1024,512]{0,1:T(8,128)(2,1)}, bf16[1024,512]{0,1:T(8,128)(2,1)S(1)}, u32[]{:S(2)}) copy-start(bf16[1024,512]{0,1:T(8,128)(2,1)S(1)} %convert_element_type.60) | copy-start | bytes 3145732
  19.9 1.3 copy-start.4
  25.1 136.5 %reduce-scatter.5.cloned.1.call-start = ((), (), s32[]{:S(2)}) async-start(), calls=%async_computation.3 | async-start | bytes 2621440 | tf_op jit(solution)/shard_map/reduce_scatter | solution.py:97
  93.1 13.2 %copy-start.2 = (f32[32,2,64,16]{3,2,1,0:T(8,128)S(1)}, f32[32,2,64,16]{3,2,1,0:T(8,128)}, u32[]{:S(2)}) copy-start(f32[32,2,64,16]{3,2,1,0:T(8,128)} %reshape_reshape.6) | copy-start | bytes 786436
  93.1 16.4 %copy-start.3 = (f32[32,2,64,16]{3,2,1,0:T(8,128)S(1)}, f32[32,2,64,16]{3,2,1,0:T(8,128)}, u32[]{:S(2)}) copy-start(f32[32,2,64,16]{3,2,1,0:T(8,128)} %reshape_reshape.7) | copy-start | bytes 786436
  117.5 176.6 %all-gather.2.cloned.1.call-start = ((), (), s32[]{:S(2)}) async-start(), calls=%async_computation.4 | async-start | bytes 1179648 | tf_op jit(solution)/shard_map/all_gather | solution.py:136
  161.5 9.9 %copy-start.11 = (bf16[8,32,64,128]{3,2,1,0:T(8,128)(2,1)S(1)}, bf16[8,32,64,128]{3,2,1,0:T(8,128)(2,1)}, u32[]{:S(2)}) copy-start(bf16[8,32,64,128]{3,2,1,0:T(8,128)(2,1)} %param.9) | copy-start | bytes 12582916
  162.8 21.8 %copy-start.7 = (f32[8,32,64]{2,0,1:T(8,128)}, f32[8,32,64]{2,0,1:T(8,128)S(1)}, u32[]{:S(2)}) copy-start(f32[8,32,64]{2,0,1:T(8,128)S(1)} %get-tuple-element.12) | copy-start | bytes 196612
  191.8 9.7 %collective-permute-start = (f32[8,2,32,64]{3,0,2,1:T(8,128)S(1)}, f32[8,2,32,64]{3,0,2,1:T(8,128)S(1)}, u32[]{:S(2)}, u32[]{:S(2)}) collective-permute-start(f32[8,2,32,64]{3,0,2,1:T(8,128)S(1)} %get-tuple-element.20), channel_id=1, source_target_pairs={{0,1},{1,2},{2,3},{3,0},{4,5},{5,6},{6,7},{7,4},{8,9},{9,10},{10,1... | collective-permute-start | bytes 393224 | tf_op jit(solution)/shard_map/ppermute | solution.py:16
  201.5 9.1 %collective-permute-start.1 = (f32[8,2,32,64]{3,0,2,1:T(8,128)S(1)}, f32[8,2,32,64]{3,0,2,1:T(8,128)}, u32[]{:S(2)}, u32[]{:S(2)}) collective-permute-start(f32[8,2,32,64]{3,0,2,1:T(8,128)S(1)} %collective-permute-done), channel_id=1, source_target_pairs={{0,1},{1,2},{2,3},{3,0},{4,5},{5,6},{6,7},{7,4},{8,9},{9,10},{10,1... | collective-permute-start | bytes 393224 | tf_op jit(solution)/shard_map/ppermute | solution.py:16
  210.6 8.4 %collective-permute-start.2 = (f32[8,2,32,64]{3,0,2,1:T(8,128)}, f32[8,2,32,64]{3,0,2,1:T(8,128)S(1)}, u32[]{:S(2)}, u32[]{:S(2)}) collective-permute-start(f32[8,2,32,64]{3,0,2,1:T(8,128)} %collective-permute-done.1), channel_id=1, source_target_pairs={{0,1},{1,2},{2,3},{3,0},{4,5},{5,6},{6,7},{7,4},{8,9},{9,10},{10,1... | collective-permute-start | bytes 393224 | tf_op jit(solution)/shard_map/ppermute | solution.py:16
  224.0 49.2 %copy-start.8 = (f32[8,32,64]{2,0,1:T(8,128)S(1)}, f32[8,32,64]{2,0,1:T(8,128)}, u32[]{:S(2)}) copy-start(f32[8,32,64]{2,0,1:T(8,128)} %copy-done.7) | copy-start | bytes 196612
  224.0 49.3 %copy-start.9 = (f32[8,4,32,64]{3,0,2,1:T(8,128)S(1)}, f32[8,4,32,64]{3,0,2,1:T(8,128)}, u32[]{:S(2)}) copy-start(f32[8,4,32,64]{3,0,2,1:T(8,128)} %reduce-scatter.5.cloned.1.call-done) | copy-start | bytes 786436
  281.9 12.2 %copy-start.6 = (bf16[1024,512]{0,1:T(8,128)(2,1)S(1)}, bf16[1024,512]{0,1:T(8,128)(2,1)}, u32[]{:S(2)}) copy-start(bf16[1024,512]{0,1:T(8,128)(2,1)} %copy-done.5) | copy-start | bytes 3145732
  298.5 5.0 %copy-start.10 = (bf16[64,64]{1,0:T(8,128)(2,1)S(1)}, bf16[64,64]{1,0:T(8,128)(2,1)}, u32[]{:S(2)}) copy-start(bf16[64,64]{1,0:T(8,128)(2,1)} %param.8) | copy-start | bytes 24580
  303.6 6.2 %copy-start.1 = (bf16[64,16,1024]{2,1,0:T(8,128)(2,1)S(1)}, bf16[64,16,1024]{2,1,0:T(8,128)(2,1)}, u32[]{:S(2)}) copy-start(bf16[64,16,1024]{2,1,0:T(8,128)(2,1)} %param.5) | copy-start | bytes 6291460
Sparse Core Ops, SparseCore 0:
  25.2 54.0 reduce-scatter.2
  117.7 43.8 reduce-scatter.4
  224.2 21.8 all-gather.1
